TPU v7x, 32 devices: a whole 2x2x4 slice. The times are simulated.
32 devices in a mesh: groups: 2 (over y), tensor: 4 (over z), dp: 4 (over x, core).
Axes of the slice: x: 2, y: 2, z: 4, core: 2. Of those that a mesh axis runs over, the one named last changes fastest.
Arguments:
- out_grad: bfloat16 [4, 1280, 4096], P('dp', ('groups', 'tensor')), parts along dimension 1, may hold values from -6 to 6
- gate_pre: bfloat16 [4, 1280, 14336], P('dp', 'groups', 'tensor'), parts along dimension 1, may hold values from -8 to 8
- up_pre: bfloat16 [4, 1280, 14336], P('dp', 'groups', 'tensor'), parts along dimension 1, may hold values from -6 to 6
- down_weight: bfloat16 [14336, 4096], P('tensor'), may hold values from -0.046875 to 0.046875
Outputs:
- gate_grad: bfloat16 [4, 1280, 14336], P('dp', 'groups', 'tensor'), parts along dimension 1
- up_grad: bfloat16 [4, 1280, 14336], P('dp', 'groups', 'tensor'), parts along dimension 1
- down_grad: bfloat16 [28672, 4096], P(('groups', 'tensor'), 'dp'), parts along dimension 0
There are 2 independent parts, one for each index of `groups`. A program takes and returns all parts, laid end to end along the dimension named above; an argument that names none is the same for every part. Nothing has to cross between parts.
All inputs are finite; a program needn't handle non-finite values.
Results may differ from a plain program's by a relative error of at most 0.014.
Values may be sent and summed in bfloat16 or wider, within the bound.
A program may use at most 128 MiB of HBM per device.

v0:
```python
import math
import jax
import jax.numpy as jnp
from jax import lax
from jax.sharding import PartitionSpec as P


def times_down(block, down_weight):
    return lax.dot_general(
        block, down_weight, (((1,), (1,)), ((), ())), preferred_element_type=jnp.float32
    )


def on_device(out_grad, gate_pre, up_pre, down_weight):
    gate = gate_pre[0].astype(jnp.float32)
    up = up_pre[0].astype(jnp.float32)
    sig = jax.nn.sigmoid(gate)
    act = gate * sig
    hidden = (act * up).astype(jnp.bfloat16)
    group_rows = hidden.shape[0]
    scale = 1.0 / math.sqrt(group_rows * lax.axis_size("dp"))
    block = lax.all_gather(out_grad, "tensor", axis=1, tiled=True)[0]
    weight_acc = jnp.einsum("tf,td->fd", hidden, block, preferred_element_type=jnp.float32)
    hidden_grad = times_down(block, down_weight)
    weight_acc, hidden_grad = (weight_acc, hidden_grad)
    down_grad = lax.psum_scatter(
        (weight_acc * scale).astype(jnp.bfloat16), "dp", scatter_dimension=1, tiled=True
    )
    gate_grad = (hidden_grad * up * sig * (1.0 + gate * (1.0 - sig))).astype(jnp.bfloat16)
    up_grad = (hidden_grad * act).astype(jnp.bfloat16)
    return (gate_grad[None], up_grad[None], down_grad)


def solution(mesh):
    return jax.shard_map(
        on_device,
        mesh=mesh,
        in_specs=(
            P("dp", ("groups", "tensor"), None),
            P("dp", "groups", "tensor"),
            P("dp", "groups", "tensor"),
            P("tensor", None),
        ),
        out_specs=(
            P("dp", "groups", "tensor"),
            P("dp", "groups", "tensor"),
            P(("groups", "tensor"), "dp"),
        ),
        check_vma=False,
    )
```

profile of v0, /device:TPU:0, one launch (start us, length us, event | category | flops | bytes accessed | tf_op | source)
XLA Modules:
  0.0 359.5 jit_solution(4585248660754477539)
XLA Ops:
  7.2 0.0 all-gather.2.cloned.1.call-start
  7.2 0.7 all-gather.2.cloned.1.call-update
  7.9 0.0 reduce-scatter.2.cloned.1.call-start
  7.9 102.4 %all-gather.2.cloned.1.call-done = bf16[1,640,4096]{2,1,0:T(8,128)(2,1)} async-done(((bf16[1,160,4096]{2,1,0:T(8,128)(2,1)}), bf16[1,640,4096]{2,1,0:T(8,128)(2,1)}) %all-gather.2.cloned.1.call-update) | async-done | bytes 5242896 | tf_op jit(solution)/shard_map/all_gather | solution.py:22
  110.4 35.9 %multiply_convert_fusion = bf16[3584,4096]{1,0:T(8,128)(2,1)} fusion(bf16[1,640,4096]{2,1,0:T(8,128)(2,1)} %all-gather.2.cloned.1.call-done, bf16[1,640,3584]{2,1,0:T(8,128)(2,1)} %param.6, bf16[1,640,3584]{2,1,0:T(8,128)(2,1)} %param.5), kind=kOutput, calls=%fused_computation | convolution fusion | flops 18838192128 | bytes 43778048 | tf_op jit(solution)/shard_map/tf,td->fd/dot_general | solution.py:23
  146.3 0.0 reduce-scatter.2.cloned.1.call-update
  146.3 34.0 %fusion.22 = (bf16[1,640,3584]{2,1,0:T(8,128)(2,1)}, bf16[1,640,3584]{2,1,0:T(8,128)(2,1)}) fusion(bf16[1,640,3584]{2,1,0:T(8,128)(2,1)} %param.5, bf16[1,640,3584]{2,1,0:T(8,128)(2,1)} %param.6, bf16[3584,4096]{1,0:T(8,128)(2,1)} %param.7, bf16[1,640,4096]{2,1,0:T(8,128)(2,1)} %all-gather.2.cloned.1.call-done), kind=kOutput, calls=%fused_computation.27 | convolution fusion | flops 18824888320 | bytes 52953088 | tf_op jit(solution)/shard_map/dot_general | solution.py:9
  180.3 172.4 %reduce-scatter.2.cloned.1.call-done = bf16[3584,1024]{1,0:T(8,128)(2,1)} async-done(((bf16[3584,4096]{1,0:T(8,128)(2,1)}), bf16[3584,1024]{1,0:T(8,128)(2,1)}) %reduce-scatter.2.cloned.1.call-update) | async-done | bytes 7340048 | tf_op jit(solution)/shard_map/reduce_scatter | solution.py:26
Async XLA Ops:
  7.2 103.2 %all-gather.2.cloned.1.call-start = ((), (), s32[]{:S(2)}) async-start(), calls=%async_computation.1 | async-start | bytes 6553600 | tf_op jit(solution)/shard_map/all_gather | solution.py:22
  7.9 344.8 %reduce-scatter.2.cloned.1.call-start = ((), (), s32[]{:S(2)}) async-start(), calls=%async_computation.2 | async-start | bytes 36700160 | tf_op jit(solution)/shard_map/reduce_scatter | solution.py:26
Sparse Core Ops, SparseCore 0:
  9.6 100.7 all-gather.1
  146.4 206.2 reduce-scatter.1
where the time goes:
time: 360 us
  waiting for transfers between devices  275 us (76%)
  matrix products  69.9 us (19%)
  between operations  14 us (4%)
    reduce_scatter x1, waiting for transfers between devices, on_device(): lax.psum_scatter((weight_acc * scale).astype(jnp.bfloat16), 'dp', scatter...  172 us
    all_gather x1, waiting for transfers between devices, on_device(): block = lax.all_gather(out_grad, 'tensor', axis=1, tiled=True)[0]  102 us
    dot_general x1, matrix products, on_device(): jnp.einsum('tf,td->fd', hidden, block, preferred_element_type=jnp.float32)  35.9 us
    dot_general x1, matrix products, times_down(): lax.dot_general(block, down_weight, (((1,), (1,)), ((), ())), preferred_e...  34 us
  transfers between devices with their start and end apart: 2, of which 2 were waited for; matrix products, arithmetic and copies ran while one was open for 9% of the time, Pallas kernels for 0%

commit v1 on v0

--- a/solution.py
+++ b/solution.py
@@ -3,6 +3,22 @@
 import jax.numpy as jnp
 from jax import lax
 from jax.sharding import PartitionSpec as P
+
+
+def collect(x, axis, dim):
+    ways, here, turn = (lax.axis_size(axis), lax.axis_index(axis), x.shape[dim])
+    dims = [n * ways if d == dim else n for d, n in enumerate(x.shape)]
+    full = lax.dynamic_update_slice_in_dim(jnp.zeros(dims, x.dtype), x, here * turn, axis=dim)
+    going_up = going_down = x
+    for far in range(1, ways // 2 + 1):
+        going_up = lax.ppermute(going_up, axis, [(d, (d + 1) % ways) for d in range(ways)])
+        full = lax.dynamic_update_slice_in_dim(full, going_up, (here - far) % ways * turn, axis=dim)
+        if 2 * far < ways:
+            going_down = lax.ppermute(going_down, axis, [(d, (d - 1) % ways) for d in range(ways)])
+            full = lax.dynamic_update_slice_in_dim(
+                full, going_down, (here + far) % ways * turn, axis=dim
+            )
+    return full
 
 
 def times_down(block, down_weight):
@@ -19,7 +35,7 @@
     hidden = (act * up).astype(jnp.bfloat16)
     group_rows = hidden.shape[0]
     scale = 1.0 / math.sqrt(group_rows * lax.axis_size("dp"))
-    block = lax.all_gather(out_grad, "tensor", axis=1, tiled=True)[0]
+    block = collect(out_grad, "tensor", 1)[0]
     weight_acc = jnp.einsum("tf,td->fd", hidden, block, preferred_element_type=jnp.float32)
     hidden_grad = times_down(block, down_weight)
     weight_acc, hidden_grad = (weight_acc, hidden_grad)

time: 360 us -> 343 us (0.953)
  waiting for transfers between devices: 275 us -> 251 us
  local copies, waits for them, and re-layouts: 0 us -> 9.05 us
  matrix products: 69.9 us -> 63.8 us
  starting transfers between devices: 0.08 us -> 5.21 us
    all_gather x1 -> x0, waiting for transfers between devices: 102 us -> none  [on_device(): block = lax.all_gather(out_grad, 'tensor', axis=1, tiled=True)[0]]
    ppermute x0 -> x3, waiting for transfers between devices: none -> 77.3 us  [the longest x2 51.5 us: collect(): lax.ppermute(going_up, axis, [(d, (d + 1) % ways) for d in range(ways)])]
    dynamic_update_slice x0 -> x4, local copies, waits for them, and re-layouts: none -> 6.1 us  [the longest x1 2.51 us: collect(): lax.dynamic_update_slice_in_dim(full, going_down, (here + far) % ways * t...]
    dot_general x1, matrix products: 35.9 us -> 30.2 us  [on_device(): jnp.einsum('tf,td->fd', hidden, block, preferred_element_type=jnp.float32)]
    ppermute x0 -> x3, starting transfers between devices: none -> 5.17 us  [the longest x2 3.08 us: collect(): lax.ppermute(going_up, axis, [(d, (d + 1) % ways) for d in range(ways)])]
  transfers between devices with their start and end apart: 2 -> 4, of which waited for: 2 -> 4; matrix products, arithmetic and copies ran while one was open for 9% -> 12% of each run, Pallas kernels for 0% -> 0%
where the time goes in v1:
time: 343 us
  waiting for transfers between devices  251 us (73%)
  matrix products  63.8 us (19%)
  between operations  14 us (4%)
  local copies, waits for them, and re-layouts  9.05 us (3%)
  starting transfers between devices  5.21 us (2%)
    reduce_scatter x1, waiting for transfers between devices, on_device(): lax.psum_scatter((weight_acc * scale).astype(jnp.bfloat16), 'dp', scatter...  174 us
    ppermute x2, waiting for transfers between devices, collect(): lax.ppermute(going_up, axis, [(d, (d + 1) % ways) for d in range(ways)])  51.5 us
    dot_general x1, matrix products, times_down(): lax.dot_general(block, down_weight, (((1,), (1,)), ((), ())), preferred_e...  33.6 us
    dot_general x1, matrix products, on_device(): jnp.einsum('tf,td->fd', hidden, block, preferred_element_type=jnp.float32)  30.2 us
    ppermute x1, waiting for transfers between devices, collect(): lax.ppermute(going_down, axis, [(d, (d - 1) % ways) for d in range(ways)])  25.8 us
  transfers between devices with their start and end apart: 4, of which 4 were waited for; matrix products, arithmetic and copies ran while one was open for 12% of the time, Pallas kernels for 0%

profile of v1, /device:TPU:0, one launch (start us, length us, event | category | flops | bytes accessed | tf_op | source)
XLA Modules:
  0.0 343.1 jit_solution(6140604258876563218)
XLA Ops:
  7.2 0.0 copy-start
  7.2 0.0 reduce-scatter.2.cloned.1.call-start
  7.2 3.1 collective-permute-start
  10.3 2.1 collective-permute-start.1
  12.4 2.9 squeeze.13
  15.3 0.0 copy-done
  15.3 0.0 slice-start
  15.3 1.2 bitcast_dynamic-update-slice_fusion.3
  16.5 0.0 slice-start.1
  16.5 25.6 %collective-permute-done = bf16[1,160,4096]{2,1,0:T(8,128)(2,1)S(1)} collective-permute-done((bf16[1,160,4096]{2,1,0:T(8,128)(2,1)}, bf16[1,160,4096]{2,1,0:T(8,128)(2,1)S(1)}, u32[]{:S(2)}, u32[]{:S(2)}) %collective-permute-start) | collective-permute-done | bytes 1310752 | tf_op jit(solution)/shard_map/ppermute | solution.py:14
  42.2 0.0 collective-permute-start.2
  42.2 1.2 bitcast_dynamic-update-slice_fusion.2
  43.4 25.8 %collective-permute-done.1 = bf16[1,160,4096]{2,1,0:T(8,128)(2,1)} collective-permute-done((bf16[1,160,4096]{2,1,0:T(8,128)(2,1)}, bf16[1,160,4096]{2,1,0:T(8,128)(2,1)}, u32[]{:S(2)}, u32[]{:S(2)}) %collective-permute-start.1) | collective-permute-done | bytes 1310752 | tf_op jit(solution)/shard_map/ppermute | solution.py:17
  69.2 2.5 bitcast_dynamic-update-slice_fusion.1
  71.7 25.9 %collective-permute-done.2 = bf16[1,160,4096]{2,1,0:T(8,128)(2,1)S(1)} collective-permute-done((bf16[1,160,4096]{2,1,0:T(8,128)(2,1)S(1)}, bf16[1,160,4096]{2,1,0:T(8,128)(2,1)S(1)}, u32[]{:S(2)}, u32[]{:S(2)}) %collective-permute-start.2) | collective-permute-done | bytes 1310752 | tf_op jit(solution)/shard_map/ppermute | solution.py:14
  97.5 1.2 bitcast_dynamic-update-slice_fusion
  98.7 0.0 slice-done
  98.7 0.0 slice-done.1
  98.7 30.2 %multiply_convert_fusion = bf16[3584,4096]{1,0:T(8,128)(2,1)} fusion(bf16[640,4096]{1,0:T(8,128)(2,1)} %bitcast_dynamic-update-slice_fusion, bf16[1,640,3584]{2,1,0:T(8,128)(2,1)} %param.6, bf16[1,640,3584]{2,1,0:T(8,128)(2,1)S(1)} %bitcast.36), kind=kOutput, calls=%fused_computation | convolution fusion | flops 18838192128 | bytes 43778048 | tf_op jit(solution)/shard_map/tf,td->fd/dot_general | solution.py:39
  128.9 0.0 reduce-scatter.2.cloned.1.call-update
  128.9 33.6 %fusion.8 = (bf16[1,640,3584]{2,1,0:T(8,128)(2,1)}, bf16[1,640,3584]{2,1,0:T(8,128)(2,1)}) fusion(bf16[1,640,3584]{2,1,0:T(8,128)(2,1)} %param.5, bf16[1,640,3584]{2,1,0:T(8,128)(2,1)} %param.6, bf16[640,4096]{1,0:T(8,128)(2,1)} %bitcast_dynamic-update-slice_fusion, bf16[3584,4096]{1,0:T(8,128)(2,1)} %param.7), kind=kOutput, calls=%fused_computation.15 | convolution fusion | flops 18824888320 | bytes 52953088 | tf_op jit(solution)/shard_map/dot_general | solution.py:25
  162.5 173.8 %reduce-scatter.2.cloned.1.call-done = bf16[3584,1024]{1,0:T(8,128)(2,1)} async-done(((bf16[3584,4096]{1,0:T(8,128)(2,1)}), bf16[3584,1024]{1,0:T(8,128)(2,1)}) %reduce-scatter.2.cloned.1.call-update) | async-done | bytes 7340048 | tf_op jit(solution)/shard_map/reduce_scatter | solution.py:42
  (1 shorter events, 0.0 us)
Async XLA Ops:
  7.2 8.2 %copy-start = (bf16[1,160,4096]{2,1,0:T(8,128)(2,1)S(1)}, bf16[1,160,4096]{2,1,0:T(8,128)(2,1)}, u32[]{:S(2)}) copy-start(bf16[1,160,4096]{2,1,0:T(8,128)(2,1)} %param.4) | copy-start | bytes 3932164
  7.2 329.1 %reduce-scatter.2.cloned.1.call-start = ((), (), s32[]{:S(2)}) async-start(), calls=%async_computation.1 | async-start | bytes 36700160 | tf_op jit(solution)/shard_map/reduce_scatter | solution.py:42
  7.2 35.0 %collective-permute-start = (bf16[1,160,4096]{2,1,0:T(8,128)(2,1)}, bf16[1,160,4096]{2,1,0:T(8,128)(2,1)S(1)}, u32[]{:S(2)}, u32[]{:S(2)}) collective-permute-start(bf16[1,160,4096]{2,1,0:T(8,128)(2,1)} %param.4), channel_id=1, source_target_pairs={{0,4},{4,8},{8,12},{12,0},{1,5},{5,9},{9,13},{13,1},{2,6},{6,10},{... | collective-permute-start | bytes 3932168 | tf_op jit(solution)/shard_map/ppermute | solution.py:14
  10.3 58.9 %collective-permute-start.1 = (bf16[1,160,4096]{2,1,0:T(8,128)(2,1)}, bf16[1,160,4096]{2,1,0:T(8,128)(2,1)}, u32[]{:S(2)}, u32[]{:S(2)}) collective-permute-start(bf16[1,160,4096]{2,1,0:T(8,128)(2,1)} %param.4), channel_id=1, source_target_pairs={{0,12},{4,0},{8,4},{12,8},{1,13},{5,1},{9,5},{13,9},{2,14},{6,2},{... | collective-permute-start | bytes 3932168 | tf_op jit(solution)/shard_map/ppermute | solution.py:17
  15.3 83.4 %slice-start = ((s8[4587520]{0:T(1024)(128)(4,1)}), s8[393216]{0:T(1024)(128)(4,1)S(1)}, s32[]{:S(2)}) async-start(s8[4587520]{0:T(1024)(128)(4,1)} %bitcast.35), calls=%async_computation.2 | async-start | bytes 786432
  16.5 82.2 %slice-start.1 = ((s8[4587520]{0:T(1024)(128)(4,1)}), s8[4194304]{0:T(1024)(128)(4,1)S(1)}, s32[]{:S(2)}) async-start(s8[4587520]{0:T(1024)(128)(4,1)} %bitcast.35), calls=%async_computation.3 | async-start | bytes 8388608
  42.2 55.3 %collective-permute-start.2 = (bf16[1,160,4096]{2,1,0:T(8,128)(2,1)S(1)}, bf16[1,160,4096]{2,1,0:T(8,128)(2,1)S(1)}, u32[]{:S(2)}, u32[]{:S(2)}) collective-permute-start(bf16[1,160,4096]{2,1,0:T(8,128)(2,1)S(1)} %collective-permute-done), channel_id=1, source_target_pairs={{0,4},{4,8},{8,12},{12,0},{1,5},{5,9},{9,13},{13,1},{2,6},{6,10},{... | collective-permute-start | bytes 3932168 | tf_op jit(solution)/shard_map/ppermute | solution.py:14
Sparse Core Ops, SparseCore 0:
  129.1 207.1 reduce-scatter.1
